TPU v7x, 32 devices: a whole 2x2x4 slice. The times are simulated.
32 devices in a mesh: lat: 4 (over y, x), lon: 8 (over z, core).
Axes of the slice: x: 2, y: 2, z: 4, core: 2. Of those that a mesh axis runs over, the one named last changes fastest.
Arguments:
- frame_one: bfloat16 [64, 256, 256], P('lat', 'lon'), may hold values from -6 to 6
- frame_two: bfloat16 [64, 256, 256], P('lat', 'lon'), may hold values from -6 to 6
- enc_weight: bfloat16 [3, 3, 256, 256], replicated, may hold values from -0.125 to 0.125
- mask_weight: bfloat16 [256, 576], replicated, may hold values from -0.375 to 0.375
Outputs:
- up_flow: float32 [2, 512, 2048], P(None, 'lat', 'lon')
All inputs are finite; a program needn't handle non-finite values.
Results may differ from a plain program's by a relative error of at most 0.0011.
Values may be sent and summed in bfloat16 or wider, within the bound.
A program may use at most 64 MiB of HBM per device.

v0:
```python
import functools
import math

import jax
import jax.numpy as jnp
from jax import lax
from jax.experimental import pallas as pl
from jax.experimental.pallas import tpu as pltpu
from jax.sharding import PartitionSpec as P

BLOCK_ROWS = 8
BLOCK_COLS = 16
BLOCK = BLOCK_ROWS * BLOCK_COLS
UPSCALE = 8
F32 = jnp.float32
BF16 = jnp.bfloat16
MESH = pl.DeviceIdType.MESH


def iota(shape, axis):
    return lax.broadcasted_iota(jnp.int32, shape, axis)


def mm(a, b):
    return jnp.dot(a, b, preferred_element_type=F32)


def mm_nt(a, b):
    return lax.dot_general(a, b, (((1,), (1,)), ((), ())), preferred_element_type=F32)


def swap_groups(xs, lane_group):
    xs = list(xs)
    for bit in (1, 2, 4):
        mask = (lane_group & bit) != 0
        shift = bit * BLOCK_COLS
        for a in range(8):
            if a & bit:
                continue
            lo, hi = xs[a], xs[a | bit]
            xs[a] = jnp.where(mask, pltpu.roll(hi, shift, 1), lo)
            xs[a | bit] = jnp.where(mask, hi, pltpu.roll(lo, BLOCK - shift, 1))
    return xs


def kernel(
    f1, f2, w_hbm, mw_hbm, out,
    fr, wv, mv, wp, acc, hal, strip_s, strip_r, corner_s, corner_r, keys, qs, mix, fb,
    lsem, ssem, rsem,
):
    rows, cols, ch = f1.shape
    rb_n, cb_n = rows // BLOCK_ROWS, cols // BLOCK_COLS
    n_mask = mw_hbm.shape[1]
    lat, lon = lax.axis_index("lat"), lax.axis_index("lon")
    nlat, nlon = lax.axis_size("lat"), lax.axis_size("lon")
    has_n, has_s = lat > 0, lat < nlat - 1
    left = (lat, lax.rem(lon + nlon - 1, nlon))
    right = (lat, lax.rem(lon + 1, nlon))
    north, south = (lat - 1, lon), (lat + 1, lon)

    loads = [
        pltpu.make_async_copy(f1, fr.at[0, pl.ds(1, rows)], lsem.at[0]),
        pltpu.make_async_copy(f2, fr.at[1, pl.ds(1, rows)], lsem.at[1]),
        pltpu.make_async_copy(w_hbm, wv, lsem.at[2]),
        pltpu.make_async_copy(mw_hbm, mv, lsem.at[3]),
    ]
    for load in loads:
        load.start()

    barrier = pltpu.get_barrier_semaphore()

    def greet(peer):
        pl.semaphore_signal(barrier, inc=1, device_id=peer, device_id_type=MESH)

    greet(left)
    greet(right)
    pl.when(has_n)(lambda: greet(north))
    pl.when(has_s)(lambda: greet(south))

    def send(k, src, dst, peer):
        return pltpu.make_async_remote_copy(
            src_ref=src, dst_ref=dst, send_sem=ssem.at[k], recv_sem=rsem.at[k],
            device_id=peer, device_id_type=MESH,
        )

    zero_row = jnp.zeros((cols, ch), BF16)
    for f in range(2):
        fr[f, 0] = zero_row
        fr[f, rows + 1] = zero_row

    halo_rows = {
        0: [send(0, f1.at[0], hal.at[1, 0], north), send(1, f2.at[0], hal.at[1, 1], north)],
        1: [
            send(2, f1.at[rows - 1], hal.at[0, 0], south),
            send(3, f2.at[rows - 1], hal.at[0, 1], south),
        ],
    }
    strips = [
        send(4, strip_s.at[0], strip_r.at[1], left),
        send(5, strip_s.at[1], strip_r.at[0], right),
    ]
    corners = [
        send(6, corner_s.at[0], corner_r.at[1], left),
        send(7, corner_s.at[1], corner_r.at[0], right),
    ]

    def absent(side):
        return jnp.logical_not(has_n if side == 0 else has_s)

    def present(side):
        return has_n if side == 0 else has_s

    for side in range(2):

        @pl.when(absent(side))
        def _():
            hal[side] = jnp.zeros(hal.shape[1:], hal.dtype)
            lo = 0 if side == 0 else BLOCK_ROWS + rows
            keys[lo : lo + BLOCK_ROWS] = jnp.zeros((BLOCK_ROWS,) + keys.shape[1:], BF16)
            at = 0 if side == 0 else rb_n + 1
            fb[at] = jnp.zeros(fb.shape[1:], F32)

    loads[0].wait()
    loads[1].wait()
    for side in range(2):
        lo, pick = (0, 0) if side == 0 else (cols - 16, 15)
        for f in range(2):
            tile = fr[f, 1 : rows + 1, lo : lo + 16, :].astype(F32)
            one = jnp.sum(jnp.where(iota(tile.shape, 1) == pick, tile, 0.0), axis=1)
            strip_s[side, f * rows : (f + 1) * rows] = one.astype(BF16)

    pl.semaphore_wait(barrier, 2 + has_n.astype(jnp.int32) + has_s.astype(jnp.int32))

    for side in range(2):

        @pl.when(present(side))
        def _():
            for copy in halo_rows[side]:
                copy.start()

    for copy in strips:
        copy.start()

    loads[2].wait()

    def col_shift(y, side):
        flat = y.reshape(-1, ch)
        n = flat.shape[0]
        turned = pltpu.roll(flat, 1 if side == 0 else n - 1, 0).reshape(y.shape)
        edge = 0 if side == 0 else cols - 1
        return jnp.where(iota(y.shape, 1) == edge, 0.0, turned)

    for f in range(2):
        lhs = jnp.concatenate(
            [fr[f, a : a + rows].reshape(rows * cols, ch) for a in range(3)], axis=1
        )
        ys = [mm(lhs, wv[:, b].reshape(3 * ch, ch)).reshape(rows, cols, ch) for b in range(3)]
        acc[f] = ys[1] + col_shift(ys[0], 0) + col_shift(ys[2], 1)

    for side in range(2):

        @pl.when(present(side))
        def _():
            for copy in halo_rows[1 - side]:
                copy.wait_recv()

    for side in range(2):
        edge = 0 if side == 0 else cols - 1
        base = 0 if side == 0 else cols - 16
        got = jnp.zeros((16, ch), F32)
        for f in range(2):
            for end in range(2):
                tile = hal[end, f, base : base + 16, :].astype(F32)
                one = tile[edge - base : edge - base + 1]
                got = jnp.where(iota((16, ch), 0) == 2 * f + end, one, got)
        corner_s[side] = got.astype(BF16)
    for copy in corners:
        copy.start()

    for side in range(2):
        a = 0 if side == 0 else 2
        r = 0 if side == 0 else rows - 1
        flat = hal[side].reshape(2 * cols, ch)
        ys = [mm(flat, wv[a, b]).reshape(2, cols, ch) for b in range(3)]
        y = ys[1] + col_shift(ys[0], 0) + col_shift(ys[2], 1)
        for f in range(2):
            acc[f, r] = acc[f, r] + y[f]

    loads[3].wait()
    p = iota((n_mask, n_mask), 0)
    want = (p - (p & 63)) + ((p & 7) << 3) + ((p >> 3) & 7)
    perm = (iota((n_mask, n_mask), 1) == want).astype(F32).astype(BF16)
    wp[...] = mm_nt(perm, mv[...]).astype(BF16)

    for copy in strips + corners:
        copy.wait_recv()
    row_id = iota((rows, ch), 0)
    for side in range(2):
        b = 0 if side == 0 else 2
        lhs = jnp.concatenate([strip_r[side], corner_r[side]], axis=0)
        z = [mm(lhs, wv[a, b]) for a in range(3)]
        for f in range(2):
            own = [z[a][f * rows : (f + 1) * rows] for a in range(3)]
            top = z[0][2 * rows + 2 * f : 2 * rows + 2 * f + 1]
            bottom = z[2][2 * rows + 2 * f + 1 : 2 * rows + 2 * f + 2]
            h = own[1] + jnp.where(row_id == 0, top, pltpu.roll(own[0], 1, 0))
            h = h + jnp.where(row_id == rows - 1, bottom, pltpu.roll(own[2], rows - 1, 0))
            lo, pick = (0, 0) if side == 0 else (cols - 8, 7)
            tile = acc[f, :, lo : lo + 8, :]
            acc[f, :, lo : lo + 8, :] = tile + jnp.where(
                iota(tile.shape, 1) == pick, h[:, None, :], 0.0
            )

    own_r = pl.ds(BLOCK_ROWS, rows)
    own_c = pl.ds(BLOCK_COLS, cols)
    keys[BLOCK_ROWS : BLOCK_ROWS + rows, BLOCK_COLS : BLOCK_COLS + cols] = acc[1].astype(BF16)

    br, bc = BLOCK_ROWS, BLOCK_COLS
    key_rows = [
        send(8, keys.at[pl.ds(br, br), own_c], keys.at[pl.ds(br + rows, br), own_c], north),
        send(9, keys.at[pl.ds(rows, br), own_c], keys.at[pl.ds(0, br), own_c], south),
    ]
    first, last = pl.ds(bc, bc), pl.ds(cols, bc)
    to_left, to_right = pl.ds(bc + cols, bc), pl.ds(0, bc)
    key_cols = [
        send(10, keys.at[own_r, first], keys.at[own_r, to_left], left),
        send(11, keys.at[own_r, last], keys.at[own_r, to_right], right),
    ]
    key_corners = {}
    for side in range(2):
        r = pl.ds(0 if side == 0 else br + rows, br)
        key_corners[side] = [
            send(12 + 2 * side, keys.at[r, first], keys.at[r, to_left], left),
            send(13 + 2 * side, keys.at[r, last], keys.at[r, to_right], right),
        ]
    for side in range(2):

        @pl.when(present(side))
        def _():
            key_rows[side].start()

    for copy in key_cols:
        copy.start()

    for cb in range(cb_n):
        for rb in range(rb_n):
            block = acc[0, rb * br : (rb + 1) * br, cb * bc : (cb + 1) * bc, :]
            qs[cb, rb * BLOCK : (rb + 1) * BLOCK] = block.astype(BF16).reshape(BLOCK, ch)

    scale = 1.0 / math.sqrt(ch)
    inside = [has_n.astype(F32), has_s.astype(F32)]
    zero = jnp.zeros((8, BLOCK), F32)
    totals = {(rb, cb): [zero, zero, zero] for rb in range(rb_n) for cb in range(cb_n)}
    sub = iota((8, BLOCK), 0).astype(F32)

    def correlate(kbs, kc):
        part = keys[kbs[0] * br : (kbs[-1] + 1) * br, kc * bc : (kc + 1) * bc, :]
        part = part.reshape(len(kbs) * BLOCK, ch)
        for cb in range(max(0, kc - 2), min(cb_n, kc + 1)):
            rbs = [rb for rb in range(rb_n) if any(0 <= kb - rb <= 2 for kb in kbs)]
            r0 = rbs[0]
            s = mm_nt(part, qs[cb, r0 * BLOCK : (rbs[-1] + 1) * BLOCK])
            for at, kb in enumerate(kbs):
                for rb in rbs:
                    if not 0 <= kb - rb <= 2:
                        continue
                    e = s[at * BLOCK : (at + 1) * BLOCK, (rb - r0) * BLOCK : (rb - r0 + 1) * BLOCK]
                    e = jnp.exp(e * scale).reshape(br, 2, 8, BLOCK)
                    lanes = [e[:, h] for h in range(2)]
                    by_row = lanes[0] + lanes[1]
                    y = by_row[0] * float(br * (kb - rb - 1))
                    for kr in range(1, br):
                        y = y + by_row[kr] * float(br * (kb - rb - 1) + kr)
                    by_col = [jnp.sum(h, axis=0) for h in lanes]
                    m = by_col[0] + by_col[1]
                    off = float(bc * (kc - cb - 1))
                    x = by_col[0] * (sub + off) + by_col[1] * (sub + (off + 8.0))
                    if kb == 0 or kb == rb_n + 1:
                        gate = inside[0] if kb == 0 else inside[1]
                        m, y, x = m * gate, y * gate, x * gate
                    old = totals[rb, cb]
                    totals[rb, cb] = [old[0] + m, old[1] + y, old[2] + x]

    own_kbs = list(range(1, rb_n + 1))
    for kc in range(1, cb_n + 1):
        correlate(own_kbs, kc)

    for cb in range(cb_n):
        logits = mm_nt(wp[...], qs[cb]).reshape(9, UPSCALE * UPSCALE, rb_n * BLOCK)
        e = jnp.exp(logits)
        mix[cb] = e / jnp.sum(e, axis=0, keepdims=True)

    for side in range(2):

        @pl.when(present(side))
        def _():
            key_rows[1 - side].wait_recv()
            for copy in key_corners[side]:
                copy.start()

    for kc in range(1, cb_n + 1):
        correlate([0], kc)
        correlate([rb_n + 1], kc)
    for copy in key_cols:
        copy.wait_recv()
    for kc in (0, cb_n + 1):
        correlate(own_kbs, kc)
    for side in range(2):

        @pl.when(present(side))
        def _():
            for copy in key_corners[side]:
                copy.wait_recv()

    for kc in (0, cb_n + 1):
        correlate([0], kc)
        correlate([rb_n + 1], kc)

    lane = iota((8, BLOCK), 1)
    sublane = iota((8, BLOCK), 0)
    qr, qc = lane >> 4, lane & 15
    for (rb, cb), (m, y, x) in totals.items():
        m, y, x = [jnp.sum(t, axis=0, keepdims=True) for t in (m, y, x)]
        fy = y / m - qr.astype(F32)
        fx = x / m - qc.astype(F32)
        both = jnp.where(sublane == 0, fy, fx) * float(UPSCALE)
        fb[rb + 1, cb + 1] = both

    flow_rows = [
        send(16, fb.at[1, pl.ds(1, cb_n)], fb.at[rb_n + 1, pl.ds(1, cb_n)], north),
        send(17, fb.at[rb_n, pl.ds(1, cb_n)], fb.at[0, pl.ds(1, cb_n)], south),
    ]
    flow_cols = [
        send(18, fb.at[pl.ds(1, rb_n), 1], fb.at[pl.ds(1, rb_n), cb_n + 1], left),
        send(19, fb.at[pl.ds(1, rb_n), cb_n], fb.at[pl.ds(1, rb_n), 0], right),
    ]
    flow_corners = {}
    for side in range(2):
        r = 0 if side == 0 else rb_n + 1
        flow_corners[side] = [
            send(20 + 2 * side, fb.at[r, 1], fb.at[r, cb_n + 1], left),
            send(21 + 2 * side, fb.at[r, cb_n], fb.at[r, 0], right),
        ]
    for side in range(2):

        @pl.when(present(side))
        def _():
            flow_rows[side].start()

    for copy in flow_cols:
        copy.start()
    for side in range(2):

        @pl.when(present(side))
        def _():
            flow_rows[1 - side].wait_recv()
            for copy in flow_corners[side]:
                copy.start()

    for copy in flow_cols:
        copy.wait_recv()
    for side in range(2):

        @pl.when(present(side))
        def _():
            for copy in flow_corners[side]:
                copy.wait_recv()

    k = iota((BLOCK, BLOCK), 0)
    weave = (iota((BLOCK, BLOCK), 1) == ((k & 15) << 3) + (k >> 4)).astype(F32).astype(BF16)

    for cb in range(cb_n):
        for rb in range(rb_n):
            shifted = {}
            for r in range(rb, rb + 3):
                mid = fb[r, cb + 1]
                shifted[r, 0] = jnp.where(
                    qc == 0, pltpu.roll(fb[r, cb], BLOCK - 15, 1), pltpu.roll(mid, 1, 1)
                )
                shifted[r, 1] = mid
                shifted[r, 2] = jnp.where(
                    qc == 15, pltpu.roll(fb[r, cb + 2], 15, 1), pltpu.roll(mid, BLOCK - 1, 1)
                )
            beside = []
            for a in range(3):
                for b in range(3):
                    here = shifted[rb + 1, b]
                    if a == 0:
                        here = pltpu.roll(jnp.where(qr == 7, shifted[rb, b], here), bc, 1)
                    if a == 2:
                        here = pltpu.roll(
                            jnp.where(qr == 0, shifted[rb + 2, b], here), BLOCK - bc, 1
                        )
                    beside.append(here)
            for d in range(2):
                up = jnp.zeros((UPSCALE * UPSCALE, BLOCK), F32)
                for n in range(9):
                    share = mix[cb, n, :, rb * BLOCK : (rb + 1) * BLOCK]
                    up = up + share * beside[n][d : d + 1]
                xs = [up[8 * j : 8 * j + 8] for j in range(8)]
                rowed = jnp.concatenate(swap_groups(xs, qr), axis=0)
                high = rowed.astype(BF16)
                rest = rowed - high.astype(F32)
                mid = rest.astype(BF16)
                low = (rest - mid.astype(F32)).astype(BF16)
                woven = mm(high, weave) + mm(mid, weave) + mm(low, weave)
                out[d, rb * 64 : (rb + 1) * 64, cb * BLOCK : (cb + 1) * BLOCK] = woven

    for side in range(2):

        @pl.when(present(side))
        def _():
            for copy in halo_rows[side] + [key_rows[side], flow_rows[side]]:
                copy.wait_send()
            for copy in key_corners[side] + flow_corners[side]:
                copy.wait_send()

    for copy in strips + corners + key_cols + flow_cols:
        copy.wait_send()


def body(frame_one, frame_two, enc_weight, mask_weight):
    rows, cols, ch = frame_one.shape
    n_mask = mask_weight.shape[1]
    rb_n, cb_n = rows // BLOCK_ROWS, cols // BLOCK_COLS
    return pl.pallas_call(
        kernel,
        out_shape=jax.ShapeDtypeStruct((2, rows * UPSCALE, cols * UPSCALE), F32),
        in_specs=[pl.BlockSpec(memory_space=pl.ANY)] * 4,
        out_specs=pl.BlockSpec(memory_space=pltpu.VMEM),
        scratch_shapes=[
            pltpu.VMEM((2, rows + 2, cols, ch), BF16),
            pltpu.VMEM(enc_weight.shape, BF16),
            pltpu.VMEM(mask_weight.shape, BF16),
            pltpu.VMEM((n_mask, ch), BF16),
            pltpu.VMEM((2, rows, cols, ch), F32),
            pltpu.VMEM((2, 2, cols, ch), BF16),
            pltpu.VMEM((2, 2 * rows, ch), BF16),
            pltpu.VMEM((2, 2 * rows, ch), BF16),
            pltpu.VMEM((2, 16, ch), BF16),
            pltpu.VMEM((2, 16, ch), BF16),
            pltpu.VMEM((rows + 2 * BLOCK_ROWS, cols + 2 * BLOCK_COLS, ch), BF16),
            pltpu.VMEM((cb_n, rb_n * BLOCK, ch), BF16),
            pltpu.VMEM((cb_n, 9, UPSCALE * UPSCALE, rb_n * BLOCK), F32),
            pltpu.VMEM((rb_n + 2, cb_n + 2, 8, BLOCK), F32),
            pltpu.SemaphoreType.DMA((4,)),
            pltpu.SemaphoreType.DMA((24,)),
            pltpu.SemaphoreType.DMA((24,)),
        ],
        compiler_params=pltpu.CompilerParams(collective_id=0, has_side_effects=True),
        name="flow",
    )(frame_one, frame_two, enc_weight, mask_weight)


def solution(mesh):
    in_specs = (P("lat", "lon", None), P("lat", "lon", None), P(), P())
    out_specs = P(None, "lat", "lon")
    return jax.shard_map(body, mesh=mesh, in_specs=in_specs, out_specs=out_specs, check_vma=False)
```

profile of v0, /device:TPU:2, one launch (start us, length us, event | category | flops | bytes accessed | tf_op | source)
XLA Modules:
  0.0 32.7 jit_solution(586464833902198657)
XLA Ops:
  0.0 1.8 %copy.5.mw_hbm = bf16[256,576]{1,0:T(8,128)(2,1)} copy(bf16[256,576]{0,1:T(8,128)(2,1)} %param.7) | data formatting | bytes 589824 | tf_op args[3]
  1.8 29.2 %flow.1 = f32[2,128,256]{2,1,0:T(8,128)} custom-call(bf16[16,32,256]{2,1,0:T(8,128)(2,1)} %f1.1, bf16[16,32,256]{2,1,0:T(8,128)(2,1)} %f2.1, bf16[3,3,256,256]{3,2,1,0:T(8,128)(2,1)} %w_hbm.1, bf16[256,576]{1,0:T(8,128)(2,1)} %copy.5.mw_hbm), custom_call_target="tpu_custom_call" | custom-call | tf_op jit(solution)/shard_map/flow/pallas_call | solution.py:426
  31.0 1.7 %copy.7 = f32[2,128,256]{2,1,0:T(8,128)} copy(f32[2,128,256]{2,1,0:T(8,128)} %flow.1) | data formatting | bytes 524288
where the time goes:
time: 32.9 us; the launch traced here: 32.7 us
  Pallas kernels  29.2 us (89%)
  local copies, waits for them, and re-layouts  3.51 us (11%)
    pallas_call x1, Pallas kernels, body(): pl.pallas_call(kernel, out_shape=jax.ShapeDtypeStruct((2, rows * UPSCALE,...  29.2 us
    unnamed x2, local copies, waits for them, and re-layouts  3.51 us

commit v1 on v0

--- a/solution.py
+++ b/solution.py
@@ -50,7 +50,7 @@
 ):
     rows, cols, ch = f1.shape
     rb_n, cb_n = rows // BLOCK_ROWS, cols // BLOCK_COLS
-    n_mask = mw_hbm.shape[1]
+    n_mask = mw_hbm.shape[0]
     lat, lon = lax.axis_index("lat"), lax.axis_index("lon")
     nlat, nlon = lax.axis_size("lat"), lax.axis_size("lon")
     has_n, has_s = lat > 0, lat < nlat - 1
@@ -190,16 +190,19 @@
     p = iota((n_mask, n_mask), 0)
     want = (p - (p & 63)) + ((p & 7) << 3) + ((p >> 3) & 7)
     perm = (iota((n_mask, n_mask), 1) == want).astype(F32).astype(BF16)
-    wp[...] = mm_nt(perm, mv[...]).astype(BF16)
+    wp[...] = mm(perm, mv[...]).astype(BF16)
 
     for copy in strips + corners:
         copy.wait_recv()
     row_id = iota((rows, ch), 0)
-    for side in range(2):
-        b = 0 if side == 0 else 2
+    rims = []
+    for side in range(2):
         lhs = jnp.concatenate([strip_r[side], corner_r[side]], axis=0)
-        z = [mm(lhs, wv[a, b]) for a in range(3)]
-        for f in range(2):
+        rims.append([mm(lhs, wv[a, 2 * side]) for a in range(3)])
+
+    def add_rim_columns(f):
+        for side in range(2):
+            z = rims[side]
             own = [z[a][f * rows : (f + 1) * rows] for a in range(3)]
             top = z[0][2 * rows + 2 * f : 2 * rows + 2 * f + 1]
             bottom = z[2][2 * rows + 2 * f + 1 : 2 * rows + 2 * f + 2]
@@ -211,14 +214,28 @@
                 iota(tile.shape, 1) == pick, h[:, None, :], 0.0
             )
 
+    add_rim_columns(1)
     own_r = pl.ds(BLOCK_ROWS, rows)
     own_c = pl.ds(BLOCK_COLS, cols)
     keys[BLOCK_ROWS : BLOCK_ROWS + rows, BLOCK_COLS : BLOCK_COLS + cols] = acc[1].astype(BF16)
 
     br, bc = BLOCK_ROWS, BLOCK_COLS
+    half = br // 2
+
+    def rows_at(start, part):
+        return pl.ds(start + part * half, half)
+
     key_rows = [
-        send(8, keys.at[pl.ds(br, br), own_c], keys.at[pl.ds(br + rows, br), own_c], north),
-        send(9, keys.at[pl.ds(rows, br), own_c], keys.at[pl.ds(0, br), own_c], south),
+        [
+            send(8 + part, keys.at[rows_at(br, part), own_c],
+                 keys.at[rows_at(br + rows, part), own_c], north)
+            for part in range(2)
+        ],
+        [
+            send(26 + part, keys.at[rows_at(rows, part), own_c],
+                 keys.at[rows_at(0, part), own_c], south)
+            for part in range(2)
+        ],
     ]
     first, last = pl.ds(bc, bc), pl.ds(cols, bc)
     to_left, to_right = pl.ds(bc + cols, bc), pl.ds(0, bc)
@@ -228,19 +245,25 @@
     ]
     key_corners = {}
     for side in range(2):
-        r = pl.ds(0 if side == 0 else br + rows, br)
-        key_corners[side] = [
-            send(12 + 2 * side, keys.at[r, first], keys.at[r, to_left], left),
-            send(13 + 2 * side, keys.at[r, last], keys.at[r, to_right], right),
-        ]
-    for side in range(2):
-
-        @pl.when(present(side))
-        def _():
-            key_rows[side].start()
+        key_corners[side] = []
+        for part in range(2):
+            r = rows_at(0 if side == 0 else br + rows, part)
+            at = 12 + 2 * side + (0 if part == 0 else 16)
+            key_corners[side] += [
+                send(at, keys.at[r, first], keys.at[r, to_left], left),
+                send(at + 1, keys.at[r, last], keys.at[r, to_right], right),
+            ]
+    for side in range(2):
+
+        @pl.when(present(side))
+        def _():
+            for copy in key_rows[side]:
+                copy.start()
 
     for copy in key_cols:
         copy.start()
+
+    add_rim_columns(0)
 
     for cb in range(cb_n):
         for rb in range(rb_n):
@@ -290,13 +313,16 @@
         e = jnp.exp(logits)
         mix[cb] = e / jnp.sum(e, axis=0, keepdims=True)
 
-    for side in range(2):
-
-        @pl.when(present(side))
-        def _():
-            key_rows[1 - side].wait_recv()
-            for copy in key_corners[side]:
+    def pass_on(side, part):
+        @pl.when(present(side))
+        def _():
+            key_rows[1 - side][part].wait_recv()
+            for copy in key_corners[side][2 * part : 2 * part + 2]:
                 copy.start()
+
+    for part in range(2):
+        for side in range(2):
+            pass_on(side, part)
 
     for kc in range(1, cb_n + 1):
         correlate([0], kc)
@@ -410,7 +436,7 @@
 
         @pl.when(present(side))
         def _():
-            for copy in halo_rows[side] + [key_rows[side], flow_rows[side]]:
+            for copy in halo_rows[side] + key_rows[side] + [flow_rows[side]]:
                 copy.wait_send()
             for copy in key_corners[side] + flow_corners[side]:
                 copy.wait_send()
@@ -431,7 +457,7 @@
         scratch_shapes=[
             pltpu.VMEM((2, rows + 2, cols, ch), BF16),
             pltpu.VMEM(enc_weight.shape, BF16),
-            pltpu.VMEM(mask_weight.shape, BF16),
+            pltpu.VMEM((n_mask, ch), BF16),
             pltpu.VMEM((n_mask, ch), BF16),
             pltpu.VMEM((2, rows, cols, ch), F32),
             pltpu.VMEM((2, 2, cols, ch), BF16),
@@ -444,12 +470,12 @@
             pltpu.VMEM((cb_n, 9, UPSCALE * UPSCALE, rb_n * BLOCK), F32),
             pltpu.VMEM((rb_n + 2, cb_n + 2, 8, BLOCK), F32),
             pltpu.SemaphoreType.DMA((4,)),
-            pltpu.SemaphoreType.DMA((24,)),
-            pltpu.SemaphoreType.DMA((24,)),
+            pltpu.SemaphoreType.DMA((32,)),
+            pltpu.SemaphoreType.DMA((32,)),
         ],
         compiler_params=pltpu.CompilerParams(collective_id=0, has_side_effects=True),
         name="flow",
-    )(frame_one, frame_two, enc_weight, mask_weight)
+    )(frame_one, frame_two, enc_weight, mask_weight.T)
 
 
 def solution(mesh):

time: 32.9 us -> 30.4 us (0.924)
  local copies, waits for them, and re-layouts: 3.51 us -> 1.67 us
  Pallas kernels: 29.2 us -> 28.5 us
    unnamed x2 -> x1, local copies, waits for them, and re-layouts: 3.51 us -> 1.67 us
    pallas_call x1, Pallas kernels: 29.2 us -> 28.5 us  [body(): pl.pallas_call(kernel, out_shape=jax.ShapeDtypeStruct((2, rows * UPSCALE,...]
where the time goes in v1:
time: 30.4 us; the launch traced here: 30.2 us
  Pallas kernels  28.5 us (94%)
  local copies, waits for them, and re-layouts  1.67 us (5%)
    pallas_call x1, Pallas kernels, body(): pl.pallas_call(kernel, out_shape=jax.ShapeDtypeStruct((2, rows * UPSCALE,...  28.5 us
    unnamed x1, local copies, waits for them, and re-layouts  1.67 us

profile of v1, /device:TPU:2, one launch (start us, length us, event | category | flops | bytes accessed | tf_op | source)
XLA Modules:
  0.0 30.2 jit_solution(7803146164486783415)
XLA Ops:
  0.0 28.5 %flow.1 = f32[2,128,256]{2,1,0:T(8,128)} custom-call(bf16[16,32,256]{2,1,0:T(8,128)(2,1)} %f1.1, bf16[16,32,256]{2,1,0:T(8,128)(2,1)} %f2.1, bf16[3,3,256,256]{3,2,1,0:T(8,128)(2,1)} %w_hbm.1, bf16[576,256]{1,0:T(8,128)(2,1)} %bitcast.1), custom_call_target="tpu_custom_call" | custom-call | tf_op jit(solution)/shard_map/flow/pallas_call | solution.py:452
  28.5 1.7 %copy.6 = f32[2,128,256]{2,1,0:T(8,128)} copy(f32[2,128,256]{2,1,0:T(8,128)} %flow.1) | data formatting | bytes 524288

commit v2 on v1

--- a/solution.py
+++ b/solution.py
@@ -186,6 +186,52 @@
         for f in range(2):
             acc[f, r] = acc[f, r] + y[f]
 
+    br, bc = BLOCK_ROWS, BLOCK_COLS
+    own_r = pl.ds(br, rows)
+    edge_w = 8
+    mid = (bc + edge_w, cols - 2 * edge_w)
+    lows, highs = (bc, edge_w), (bc + cols - edge_w, edge_w)
+
+    def key_row_sends(k, span):
+        c = pl.ds(*span)
+        return [
+            send(k, keys.at[pl.ds(br, br), c], keys.at[pl.ds(br + rows, br), c], north),
+            send(k + 1, keys.at[pl.ds(rows, br), c], keys.at[pl.ds(0, br), c], south),
+        ]
+
+    def key_col_sends(k, r, early):
+        off = edge_w if early else 0
+        back = 0 if early else edge_w
+        return [
+            send(k, keys.at[r, pl.ds(bc + off, edge_w)],
+                 keys.at[r, pl.ds(bc + cols + off, edge_w)], left),
+            send(k + 1, keys.at[r, pl.ds(cols + back, edge_w)],
+                 keys.at[r, pl.ds(back, edge_w)], right),
+        ]
+
+    rows_mid = key_row_sends(8, mid)
+    rows_low = key_row_sends(10, lows)
+    rows_high = key_row_sends(12, highs)
+    cols_early = key_col_sends(14, own_r, True)
+    cols_late = key_col_sends(24, own_r, False)
+    corners_early, corners_late = {}, {}
+    for side in range(2):
+        r = pl.ds(0 if side == 0 else br + rows, br)
+        corners_early[side] = key_col_sends(26 + 4 * side, r, True)
+        corners_late[side] = key_col_sends(28 + 4 * side, r, False)
+
+    keys[br : br + rows, mid[0] : mid[0] + mid[1]] = acc[
+        1, :, edge_w : cols - edge_w, :
+    ].astype(BF16)
+    for side in range(2):
+
+        @pl.when(present(side))
+        def _():
+            rows_mid[side].start()
+
+    for copy in cols_early:
+        copy.start()
+
     loads[3].wait()
     p = iota((n_mask, n_mask), 0)
     want = (p - (p & 63)) + ((p & 7) << 3) + ((p >> 3) & 7)
@@ -215,52 +261,18 @@
             )
 
     add_rim_columns(1)
-    own_r = pl.ds(BLOCK_ROWS, rows)
-    own_c = pl.ds(BLOCK_COLS, cols)
-    keys[BLOCK_ROWS : BLOCK_ROWS + rows, BLOCK_COLS : BLOCK_COLS + cols] = acc[1].astype(BF16)
-
-    br, bc = BLOCK_ROWS, BLOCK_COLS
-    half = br // 2
-
-    def rows_at(start, part):
-        return pl.ds(start + part * half, half)
-
-    key_rows = [
-        [
-            send(8 + part, keys.at[rows_at(br, part), own_c],
-                 keys.at[rows_at(br + rows, part), own_c], north)
-            for part in range(2)
-        ],
-        [
-            send(26 + part, keys.at[rows_at(rows, part), own_c],
-                 keys.at[rows_at(0, part), own_c], south)
-            for part in range(2)
-        ],
-    ]
-    first, last = pl.ds(bc, bc), pl.ds(cols, bc)
-    to_left, to_right = pl.ds(bc + cols, bc), pl.ds(0, bc)
-    key_cols = [
-        send(10, keys.at[own_r, first], keys.at[own_r, to_left], left),
-        send(11, keys.at[own_r, last], keys.at[own_r, to_right], right),
-    ]
-    key_corners = {}
-    for side in range(2):
-        key_corners[side] = []
-        for part in range(2):
-            r = rows_at(0 if side == 0 else br + rows, part)
-            at = 12 + 2 * side + (0 if part == 0 else 16)
-            key_corners[side] += [
-                send(at, keys.at[r, first], keys.at[r, to_left], left),
-                send(at + 1, keys.at[r, last], keys.at[r, to_right], right),
-            ]
-    for side in range(2):
-
-        @pl.when(present(side))
-        def _():
-            for copy in key_rows[side]:
-                copy.start()
-
-    for copy in key_cols:
+    for lo in (0, cols - edge_w):
+        keys[br : br + rows, bc + lo : bc + lo + edge_w] = acc[
+            1, :, lo : lo + edge_w, :
+        ].astype(BF16)
+    for side in range(2):
+
+        @pl.when(present(side))
+        def _():
+            rows_low[side].start()
+            rows_high[side].start()
+
+    for copy in cols_late:
         copy.start()
 
     add_rim_columns(0)
@@ -308,26 +320,29 @@
     for kc in range(1, cb_n + 1):
         correlate(own_kbs, kc)
 
+    def pass_on(arrivals, relays):
+        for side in range(2):
+
+            @pl.when(present(side))
+            def _():
+                for rows_sent in arrivals:
+                    rows_sent[1 - side].wait_recv()
+                for copy in relays[side]:
+                    copy.start()
+
+    pass_on([rows_mid], corners_early)
+
     for cb in range(cb_n):
         logits = mm_nt(wp[...], qs[cb]).reshape(9, UPSCALE * UPSCALE, rb_n * BLOCK)
         e = jnp.exp(logits)
         mix[cb] = e / jnp.sum(e, axis=0, keepdims=True)
 
-    def pass_on(side, part):
-        @pl.when(present(side))
-        def _():
-            key_rows[1 - side][part].wait_recv()
-            for copy in key_corners[side][2 * part : 2 * part + 2]:
-                copy.start()
-
-    for part in range(2):
-        for side in range(2):
-            pass_on(side, part)
+    pass_on([rows_low, rows_high], corners_late)
 
     for kc in range(1, cb_n + 1):
         correlate([0], kc)
         correlate([rb_n + 1], kc)
-    for copy in key_cols:
+    for copy in cols_early + cols_late:
         copy.wait_recv()
     for kc in (0, cb_n + 1):
         correlate(own_kbs, kc)
@@ -335,7 +350,7 @@
 
         @pl.when(present(side))
         def _():
-            for copy in key_corners[side]:
+            for copy in corners_early[side] + corners_late[side]:
                 copy.wait_recv()
 
     for kc in (0, cb_n + 1):
@@ -436,12 +451,14 @@
 
         @pl.when(present(side))
         def _():
-            for copy in halo_rows[side] + key_rows[side] + [flow_rows[side]]:
+            for copy in halo_rows[side] + [
+                rows_mid[side], rows_low[side], rows_high[side], flow_rows[side]
+            ]:
                 copy.wait_send()
-            for copy in key_corners[side] + flow_corners[side]:
+            for copy in corners_early[side] + corners_late[side] + flow_corners[side]:
                 copy.wait_send()
 
-    for copy in strips + corners + key_cols + flow_cols:
+    for copy in strips + corners + cols_early + cols_late + flow_cols:
         copy.wait_send()
 
 
@@ -470,8 +487,8 @@
             pltpu.VMEM((cb_n, 9, UPSCALE * UPSCALE, rb_n * BLOCK), F32),
             pltpu.VMEM((rb_n + 2, cb_n + 2, 8, BLOCK), F32),
             pltpu.SemaphoreType.DMA((4,)),
-            pltpu.SemaphoreType.DMA((32,)),
-            pltpu.SemaphoreType.DMA((32,)),
+            pltpu.SemaphoreType.DMA((34,)),
+            pltpu.SemaphoreType.DMA((34,)),
         ],
         compiler_params=pltpu.CompilerParams(collective_id=0, has_side_effects=True),
         name="flow",

time: 30.4 us -> 27.9 us (0.918)
  the two profiles are of different devices: /device:TPU:2 before, /device:TPU:0 now
where the time goes in v2:
time: 27.9 us; the launch traced here: 27.7 us
  Pallas kernels  26 us (93%)
  local copies, waits for them, and re-layouts  1.67 us (6%)
    pallas_call x1, Pallas kernels, body(): pl.pallas_call(kernel, out_shape=jax.ShapeDtypeStruct((2, rows * UPSCALE,...  26 us
    unnamed x1, local copies, waits for them, and re-layouts  1.67 us

profile of v2, /device:TPU:0, one launch (start us, length us, event | category | flops | bytes accessed | tf_op | source)
XLA Modules:
  0.0 27.7 jit_solution(17483043153049341611)
XLA Ops:
  0.0 26.0 %flow.1 = f32[2,128,256]{2,1,0:T(8,128)} custom-call(bf16[16,32,256]{2,1,0:T(8,128)(2,1)} %f1.1, bf16[16,32,256]{2,1,0:T(8,128)(2,1)} %f2.1, bf16[3,3,256,256]{3,2,1,0:T(8,128)(2,1)} %w_hbm.1, bf16[576,256]{1,0:T(8,128)(2,1)} %bitcast.1), custom_call_target="tpu_custom_call" | custom-call | tf_op jit(solution)/shard_map/flow/pallas_call | solution.py:469
  26.0 1.7 %copy.6 = f32[2,128,256]{2,1,0:T(8,128)} copy(f32[2,128,256]{2,1,0:T(8,128)} %flow.1) | data formatting | bytes 524288

commit v3 on v2

--- a/solution.py
+++ b/solution.py
@@ -377,34 +377,28 @@
     ]
     flow_corners = {}
     for side in range(2):
-        r = 0 if side == 0 else rb_n + 1
+        src_r, dst_r = (1, rb_n + 1) if side == 0 else (rb_n, 0)
+        to = lat - 1 if side == 0 else lat + 1
         flow_corners[side] = [
-            send(20 + 2 * side, fb.at[r, 1], fb.at[r, cb_n + 1], left),
-            send(21 + 2 * side, fb.at[r, cb_n], fb.at[r, 0], right),
+            send(20 + 2 * side, fb.at[src_r, 1], fb.at[dst_r, cb_n + 1], (to, left[1])),
+            send(21 + 2 * side, fb.at[src_r, cb_n], fb.at[dst_r, 0], (to, right[1])),
         ]
     for side in range(2):
 
         @pl.when(present(side))
         def _():
-            flow_rows[side].start()
+            for copy in flow_corners[side] + [flow_rows[side]]:
+                copy.start()
 
     for copy in flow_cols:
         copy.start()
-    for side in range(2):
-
-        @pl.when(present(side))
-        def _():
-            flow_rows[1 - side].wait_recv()
-            for copy in flow_corners[side]:
-                copy.start()
-
     for copy in flow_cols:
         copy.wait_recv()
     for side in range(2):
 
         @pl.when(present(side))
         def _():
-            for copy in flow_corners[side]:
+            for copy in flow_corners[1 - side] + [flow_rows[1 - side]]:
                 copy.wait_recv()
 
     k = iota((BLOCK, BLOCK), 0)

time: 27.9 us -> 26.5 us (0.950)
  Pallas kernels: 26 us -> 24.7 us
    pallas_call x1, Pallas kernels: 26 us -> 24.7 us  [body(): pl.pallas_call(kernel, out_shape=jax.ShapeDtypeStruct((2, rows * UPSCALE,...]
where the time goes in v3:
time: 26.5 us; the launch traced here: 26.4 us
  Pallas kernels  24.7 us (93%)
  local copies, waits for them, and re-layouts  1.67 us (6%)
    pallas_call x1, Pallas kernels, body(): pl.pallas_call(kernel, out_shape=jax.ShapeDtypeStruct((2, rows * UPSCALE,...  24.7 us
    unnamed x1, local copies, waits for them, and re-layouts  1.67 us

profile of v3, /device:TPU:0, one launch (start us, length us, event | category | flops | bytes accessed | tf_op | source)
XLA Modules:
  0.0 26.4 jit_solution(18329129102696387468)
XLA Ops:
  0.0 24.7 %flow.1 = f32[2,128,256]{2,1,0:T(8,128)} custom-call(bf16[16,32,256]{2,1,0:T(8,128)(2,1)} %f1.1, bf16[16,32,256]{2,1,0:T(8,128)(2,1)} %f2.1, bf16[3,3,256,256]{3,2,1,0:T(8,128)(2,1)} %w_hbm.1, bf16[576,256]{1,0:T(8,128)(2,1)} %bitcast.1), custom_call_target="tpu_custom_call" | custom-call | tf_op jit(solution)/shard_map/flow/pallas_call | solution.py:463
  24.7 1.7 %copy.6 = f32[2,128,256]{2,1,0:T(8,128)} copy(f32[2,128,256]{2,1,0:T(8,128)} %flow.1) | data formatting | bytes 524288

commit v4 on v3

--- a/solution.py
+++ b/solution.py
@@ -192,11 +192,11 @@
     mid = (bc + edge_w, cols - 2 * edge_w)
     lows, highs = (bc, edge_w), (bc + cols - edge_w, edge_w)
 
-    def key_row_sends(k, span):
+    def key_row_sends(k, span, at=0, n=br):
         c = pl.ds(*span)
         return [
-            send(k, keys.at[pl.ds(br, br), c], keys.at[pl.ds(br + rows, br), c], north),
-            send(k + 1, keys.at[pl.ds(rows, br), c], keys.at[pl.ds(0, br), c], south),
+            send(k, keys.at[pl.ds(br + at, n), c], keys.at[pl.ds(br + rows + at, n), c], north),
+            send(k + 1, keys.at[pl.ds(rows + at, n), c], keys.at[pl.ds(at, n), c], south),
         ]
 
     def key_col_sends(k, r, early):
@@ -210,15 +210,21 @@
         ]
 
     rows_mid = key_row_sends(8, mid)
-    rows_low = key_row_sends(10, lows)
-    rows_high = key_row_sends(12, highs)
+    half = br // 2
+    rows_edge = [
+        [key_row_sends(10, lows, 0, half), key_row_sends(12, highs, 0, half)],
+        [key_row_sends(34, lows, half, half), key_row_sends(36, highs, half, half)],
+    ]
     cols_early = key_col_sends(14, own_r, True)
     cols_late = key_col_sends(24, own_r, False)
-    corners_early, corners_late = {}, {}
+    corners_early, corners_late = {}, [{}, {}]
     for side in range(2):
         r = pl.ds(0 if side == 0 else br + rows, br)
         corners_early[side] = key_col_sends(26 + 4 * side, r, True)
-        corners_late[side] = key_col_sends(28 + 4 * side, r, False)
+        for part in range(2):
+            r = pl.ds((0 if side == 0 else br + rows) + part * half, half)
+            k = 28 + 4 * side if part == 0 else 38 + 2 * side
+            corners_late[part][side] = key_col_sends(k, r, False)
 
     keys[br : br + rows, mid[0] : mid[0] + mid[1]] = acc[
         1, :, edge_w : cols - edge_w, :
@@ -269,8 +275,9 @@
 
         @pl.when(present(side))
         def _():
-            rows_low[side].start()
-            rows_high[side].start()
+            for part in rows_edge:
+                for rows_sent in part:
+                    rows_sent[side].start()
 
     for copy in cols_late:
         copy.start()
@@ -337,7 +344,8 @@
         e = jnp.exp(logits)
         mix[cb] = e / jnp.sum(e, axis=0, keepdims=True)
 
-    pass_on([rows_low, rows_high], corners_late)
+    for part in range(2):
+        pass_on(rows_edge[part], corners_late[part])
 
     for kc in range(1, cb_n + 1):
         correlate([0], kc)
@@ -350,7 +358,7 @@
 
         @pl.when(present(side))
         def _():
-            for copy in corners_early[side] + corners_late[side]:
+            for copy in corners_early[side] + corners_late[0][side] + corners_late[1][side]:
                 copy.wait_recv()
 
     for kc in (0, cb_n + 1):
@@ -446,10 +454,10 @@
         @pl.when(present(side))
         def _():
             for copy in halo_rows[side] + [
-                rows_mid[side], rows_low[side], rows_high[side], flow_rows[side]
-            ]:
+                rows_mid[side], flow_rows[side]
+            ] + [sent[side] for part in rows_edge for sent in part]:
                 copy.wait_send()
-            for copy in corners_early[side] + corners_late[side] + flow_corners[side]:
+            for copy in corners_early[side] + corners_late[0][side] + corners_late[1][side] + flow_corners[side]:
                 copy.wait_send()
 
     for copy in strips + corners + cols_early + cols_late + flow_cols:
@@ -481,8 +489,8 @@
             pltpu.VMEM((cb_n, 9, UPSCALE * UPSCALE, rb_n * BLOCK), F32),
             pltpu.VMEM((rb_n + 2, cb_n + 2, 8, BLOCK), F32),
             pltpu.SemaphoreType.DMA((4,)),
-            pltpu.SemaphoreType.DMA((34,)),
-            pltpu.SemaphoreType.DMA((34,)),
+            pltpu.SemaphoreType.DMA((42,)),
+            pltpu.SemaphoreType.DMA((42,)),
         ],
         compiler_params=pltpu.CompilerParams(collective_id=0, has_side_effects=True),
         name="flow",

time: 26.5 us -> 26.5 us (level)
  no operation moved by 1% of the time
where the time goes in v4:
time: 26.5 us; the launch traced here: 26.4 us
  Pallas kernels  24.7 us (93%)
  local copies, waits for them, and re-layouts  1.67 us (6%)
    pallas_call x1, Pallas kernels, body(): pl.pallas_call(kernel, out_shape=jax.ShapeDtypeStruct((2, rows * UPSCALE,...  24.7 us
    unnamed x1, local copies, waits for them, and re-layouts  1.67 us

profile of v4, /device:TPU:0, one launch (start us, length us, event | category | flops | bytes accessed | tf_op | source)
XLA Modules:
  0.0 26.4 jit_solution(7297645026539484750)
XLA Ops:
  0.0 24.7 %flow.1 = f32[2,128,256]{2,1,0:T(8,128)} custom-call(bf16[16,32,256]{2,1,0:T(8,128)(2,1)} %f1.1, bf16[16,32,256]{2,1,0:T(8,128)(2,1)} %f2.1, bf16[3,3,256,256]{3,2,1,0:T(8,128)(2,1)} %w_hbm.1, bf16[576,256]{1,0:T(8,128)(2,1)} %bitcast.1), custom_call_target="tpu_custom_call" | custom-call | tf_op jit(solution)/shard_map/flow/pallas_call | solution.py:471
  24.7 1.7 %copy.6 = f32[2,128,256]{2,1,0:T(8,128)} copy(f32[2,128,256]{2,1,0:T(8,128)} %flow.1) | data formatting | bytes 524288
